TPU v7x, 32 devices: a whole 2x2x4 slice. The times are simulated.
32 devices in a mesh: row: 16 (over z, y, core), col: 2 (over x).
Axes of the slice: x: 2, y: 2, z: 4, core: 2. Of those that a mesh axis runs over, the one named last changes fastest.
Arguments:
- seq: float32 [768, 1024], P('row', 'col'), may hold values from -6 to 6
- query: float32 [768, 1024], P('row', 'col'), may hold values from -24 to 24, as said below
- key: float32 [768, 1024], P('col', 'row'), may hold values from -24 to 24, as said below
- value: float32 [768, 1024], P('col', 'row'), may hold values from -6 to 6
- pair: float32 [768, 768, 128], P('row', 'col'), may hold values from -6 to 6
- w_bias: float32 [128, 32], replicated, may hold values from -0.5 to 0.5
- w_out: float32 [1024, 1024], P(None, 'col'), may hold values from -0.75 to 0.75
- w_left: float32 [1024, 64], P('col'), may hold values from -0.1875 to 0.1875
- w_right: float32 [1024, 64], P('col'), may hold values from -0.1875 to 0.1875
- w_outer: float32 [128, 128], replicated, may hold values from -0.5 to 0.5
- outer_bias: float32 [128], replicated, may hold values from -3 to 3
- w_up: float32 [128, 512], replicated, may hold values from -0.5 to 0.5
- w_down: float32 [512, 128], replicated, may hold values from -0.25 to 0.25
Outputs:
- seq_new: float32 [768, 1024], P('row', 'col')
- pair_new: float32 [768, 768, 128], P('row', 'col')
Inputs may be any that keep to these rules, and one draw needn't show every extreme that they name: `query`: Head-major queries of order one; some residues may be much larger. `key`: Head-major keys of order one; some residues may be much larger.
All inputs are finite; a program needn't handle non-finite values.
Results may differ from a plain program's by a relative error of at most 0.0003.
Values sent between devices are 32-bit elements; how exact they have to be, the bound alone decides.
A program may use at most 128 MiB of HBM per device.

v0:
```python
import jax
import jax.numpy as jnp
from jax import lax
from jax.sharding import PartitionSpec as P

HIGH = lax.Precision.HIGHEST


def merged(x, axis, combine):
    everything = jax.tree.map(lambda part: lax.all_gather(part, axis), x)
    leading = jax.tree.map(lambda part: part[0], everything)

    def hop(k, so_far):
        return combine(so_far, jax.tree.map(lambda part: part[k], everything))

    return lax.fori_loop(1, lax.axis_size(axis), hop, leading)


def channel_norm(x):
    centre = x - jnp.mean(x, axis=-1, keepdims=True)
    return centre * lax.rsqrt(jnp.mean(centre * centre, axis=-1, keepdims=True) + 1e-05)


def combine(first, second):
    top = jnp.maximum(first[0], second[0])
    scale_one = jnp.exp(first[0] - top)
    scale_two = jnp.exp(second[0] - top)
    totals = first[1] * scale_one + second[1] * scale_two
    weighted = first[2] * scale_one[..., None] + second[2] * scale_two[..., None]
    return (top, totals, weighted)


def partial_softmax(q_heads, k_heads, v_heads, bias, scale):
    scores = jnp.einsum("ihd,jhd->ihj", q_heads, k_heads, precision=HIGH) * scale + bias
    top = jnp.max(scores, axis=2)
    expo = jnp.exp(scores - top[..., None])
    totals = jnp.sum(expo, axis=2)
    weighted = jnp.einsum("ihj,jhd->ihd", expo, v_heads, precision=HIGH)
    return (top, totals, weighted)


def per_device(
    seq, query, key, value, pair, w_bias, w_out, w_left, w_right, w_outer, outer_bias, w_up, w_down
):
    rows_here = pair.shape[0]
    cols_here = pair.shape[1]
    channels = pair.shape[2]
    heads = w_bias.shape[1]
    width = w_out.shape[0]
    head_dim = width // heads
    proj_width = w_left.shape[1]
    scale = 1.0 / jnp.sqrt(jnp.float32(head_dim))
    bias = jnp.einsum("ijc,ch->ihj", channel_norm(pair), w_bias, precision=HIGH)
    queries = lax.all_gather(query, "col", axis=1, tiled=True)
    keys_all, values_all = (
        lax.all_gather(key, "row", axis=1, tiled=True),
        lax.all_gather(value, "row", axis=1, tiled=True),
    )
    parts = partial_softmax(
        queries.reshape(rows_here, heads, head_dim),
        keys_all.reshape(cols_here, heads, head_dim),
        values_all.reshape(cols_here, heads, head_dim),
        bias,
        scale,
    )
    top, totals, weighted = merged(parts, "col", combine)
    attn = (weighted / totals[..., None]).reshape(rows_here, width)
    seq_new = seq + jnp.dot(attn, w_out, precision=HIGH)
    sum_value, sum_square = lax.psum(
        (jnp.sum(seq_new, axis=1), jnp.sum(seq_new * seq_new, axis=1)), "col"
    )
    mean_value = (sum_value / width)[:, None]
    mean_square = (sum_square / width)[:, None]
    seq_norm = (seq_new - mean_value) * lax.rsqrt(mean_square - mean_value * mean_value + 1e-05)
    left_part = jnp.dot(seq_norm, w_left, precision=HIGH)
    right_part = jnp.dot(seq_norm, w_right, precision=HIGH)
    left, right = lax.psum((left_part, right_part), "col")
    right_every = lax.all_gather(right, "row", axis=0, tiled=True)
    start = lax.axis_index("col") * cols_here
    right_block = lax.dynamic_slice_in_dim(right_every, start, cols_here, 0)
    w_prod = w_outer[:proj_width]
    w_diff = w_outer[proj_width:]
    table = right_block[:, :, None] * w_prod[None, :, :]
    left_diff = jnp.dot(left, w_diff, precision=HIGH)
    right_diff = jnp.dot(right_block, w_diff, precision=HIGH)
    outer = (
        jnp.einsum("ip,jpc->ijc", left, table, precision=HIGH)
        + left_diff[:, None, :]
        - right_diff[None, :, :]
        + outer_bias
    )
    pair_mid = pair + outer
    flat = pair_mid.reshape(rows_here * cols_here, channels)
    hidden_act = jax.nn.relu(jnp.dot(channel_norm(flat), w_up, precision=HIGH))
    pair_new = flat + jnp.dot(hidden_act, w_down, precision=HIGH)
    return (seq_new, pair_new.reshape(rows_here, cols_here, channels))


def solution(mesh):
    in_specs = (
        P("row", "col"),
        P("row", "col"),
        P("col", "row"),
        P("col", "row"),
        P("row", "col", None),
        P(),
        P(None, "col"),
        P("col", None),
        P("col", None),
        P(),
        P(),
        P(),
        P(),
    )
    out_specs = (P("row", "col"), P("row", "col", None))
    return jax.shard_map(
        per_device, mesh=mesh, in_specs=in_specs, out_specs=out_specs, check_vma=False
    )
```

profile of v0, /device:TPU:0, one launch (start us, length us, event | category | flops | bytes accessed | tf_op | source)
XLA Modules:
  0.0 295.0 jit_solution(9783816739350070599)
XLA Ops:
  7.2 0.0 copy-start
  7.2 0.0 all-gather.8.cloned.1.call-start
  7.2 0.7 all-gather.8.cloned.1.call-update
  7.9 0.0 all-gather.10.cloned.1.call-start
  8.0 0.7 all-gather.10.cloned.1.call-update
  8.7 6.7 %all_gather.31 = f32[48,1024]{1,0:T(8,128)S(1)} all-gather(f32[48,512]{1,0:T(8,128)} %param.14), channel_id=1, replica_groups=mesh['row'=16,'col'=2] {'col'}, dimensions={1}, use_global_device_ids=true | all-gather | bytes 294912 | tf_op jit(solution)/shard_map/all_gather | solution.py:54
  15.4 0.2 copy.49
  15.6 0.0 copy-start.7
  15.6 6.2 %reduce_sum.63 = f32[48,384]{1,0:T(8,128)S(1)} reduce(f32[48,384,128]{2,1,0:T(8,128)} %param.17, f32[]{:T(128)} %constant.13.clone.1), dimensions={2}, to_apply=%region_0.0 | reduce | flops 2340864 | bytes 9510916 | tf_op jit(solution)/shard_map/reduce_sum | solution.py:20
  21.8 7.7 %multiply_reduce_fusion.1 = f32[48,384]{1,0:T(8,128)S(1)} fusion(f32[48,384,128]{2,1,0:T(8,128)} %param.17, f32[48,384]{1,0:T(8,128)S(1)} %broadcast_multiply_fusion.1), kind=kLoop, calls=%fused_computation.12 | loop fusion | flops 7059456 | bytes 9584640 | tf_op jit(solution)/shard_map/reduce_sum | solution.py:21
  29.5 0.0 copy-done.7
  29.5 15.9 %fusion.9 = f32[48,384,32]{1,2,0:T(8,128)} fusion(f32[48,384,128]{2,1,0:T(8,128)} %param.17, f32[48,384]{1,0:T(8,128)S(1)} %add_rsqrt_fusion.1, f32[48,384]{1,0:T(8,128)S(1)} %broadcast_multiply_fusion.1, f32[128,32]{0,1:T(8,128)S(1)} %copy-done.7), kind=kOutput, calls=%fused_computation.10 | convolution fusion | flops 910688256 | bytes 11960320 | tf_op jit(solution)/shard_map/ijc,ch->ihj/dot_general | solution.py:53
  45.4 7.2 %all-gather.8.cloned.1.call-done = f32[384,1024]{0,1:T(8,128)} async-done(((f32[384,64]{0,1:T(8,128)}), f32[384,1024]{0,1:T(8,128)}) %all-gather.8.cloned.1.call-update) | async-done | bytes 1572880 | tf_op jit(solution)/shard_map/all_gather | solution.py:56
  52.6 5.7 %fusion.45 = (f32[48,32]{0,1:T(8,128)S(1)}, f32[48,32,384]{2,0,1:T(8,128)S(1)}) fusion(f32[48,384,32]{1,2,0:T(8,128)} %fusion.9, f32[384,32,32]{0,2,1:T(8,128)} %bitcast.72, f32[48,32,32]{0,2,1:T(8,128)S(1)} %bitcast.70), kind=kOutput, calls=%fused_computation.63 | convolution fusion | flops 228260352 | bytes 6494208 | tf_op jit(solution)/shard_map/ihd,jhd->ihj/dot_general | solution.py:34
  58.3 0.0 copy-start.4
  58.3 0.0 slice-start.6
  58.3 1.4 copy-done.2
  59.7 0.8 fusion.18
  60.5 32.7 %all-gather.10.cloned.1.call-done = f32[384,1024]{0,1:T(8,128)} async-done(((f32[384,64]{0,1:T(8,128)}), f32[384,1024]{0,1:T(8,128)}) %all-gather.10.cloned.1.call-update) | async-done | bytes 1572880 | tf_op jit(solution)/shard_map/all_gather | solution.py:57
  93.3 5.1 %fusion.20 = f32[48,32,32]{0,2,1:T(8,128)S(1)} fusion(f32[384,32,32]{0,2,1:T(8,128)} %bitcast.71, f32[48,32,384]{2,0,1:T(8,128)} %copy-done.2, f32[48,32]{0,1:T(8,128)S(1)} %get-tuple-element.37), kind=kOutput, calls=%fused_computation.22 | convolution fusion | flops 227082240 | bytes 4134912 | tf_op jit(solution)/shard_map/ihj,jhd->ihd/dot_general | solution.py:38
  98.3 4.4 %all-gather.3 = f32[2,48,32]{1,2,0:T(8,128)S(1)} all-gather(f32[1,48,32]{1,2,0:T(8,128)S(1)} %bitcast.73), channel_id=3, replica_groups=mesh['row'=16,'col'=2] {'col'}, dimensions={0}, use_global_device_ids=true | all-gather | bytes 18432 | tf_op jit(solution)/shard_map/all_gather | solution.py:10
  102.8 4.4 %all-gather.4 = f32[2,48,32]{1,2,0:T(8,128)S(1)} all-gather(f32[1,48,32]{1,2,0:T(8,128)S(1)} %bitcast.74), channel_id=4, replica_groups=mesh['row'=16,'col'=2] {'col'}, dimensions={0}, use_global_device_ids=true | all-gather | bytes 18432 | tf_op jit(solution)/shard_map/all_gather | solution.py:10
  107.2 0.1 copy.54
  107.2 0.1 copy.52
  107.3 0.7 copy.53
  108.0 0.7 copy.51
  108.7 0.0 copy-start.8
  108.7 18.0 %all-gather = f32[96,32,32]{2,1,0:T(8,128)S(1)} all-gather(f32[48,32,32]{2,1,0:T(8,128)S(1)} %copy.51), channel_id=2, replica_groups=mesh['row'=16,'col'=2] {'col'}, dimensions={0}, use_global_device_ids=true | all-gather | bytes 589824 | tf_op jit(solution)/shard_map/all_gather | solution.py:10
  126.8 2.0 fusion.23
  128.8 0.4 reshape.150
  129.2 0.0 copy-done
  129.2 2.3 fusion.42
  131.5 0.0 copy-start.3
  131.5 4.9 %all-reduce.1 = (f32[48]{0:T(128)S(1)}, f32[48]{0:T(128)S(1)}) all-reduce(f32[48]{0:T(128)S(1)} %get-tuple-element.19, f32[48]{0:T(128)S(1)} %get-tuple-element.18), channel_id=1, replica_groups=mesh['row'=16,'col'=2] {'col'}, use_global_device_ids=true, to_apply=%region_7.0 | all-reduce | flops 96 | bytes 768 | tf_op jit(solution)/shard_map/psum | solution.py:69
  136.5 1.2 fusion.24
  137.7 1.2 fusion.25
  138.9 8.6 %all-reduce = (f32[48,64]{1,0:T(8,128)S(1)}, f32[48,64]{1,0:T(8,128)S(1)}) all-reduce(f32[48,64]{1,0:T(8,128)S(1)} %fusion.24, f32[48,64]{1,0:T(8,128)S(1)} %fusion.25), channel_id=1, replica_groups=mesh['row'=16,'col'=2] {'col'}, use_global_device_ids=true, to_apply=%region_9.0 | all-reduce | flops 6144 | bytes 49152 | tf_op jit(solution)/shard_map/psum | solution.py:77
  147.5 0.0 copy-done.4
  147.5 0.2 fusion.32
  147.6 20.2 %all_gather.39 = f32[768,64]{1,0:T(8,128)S(1)} all-gather(f32[48,64]{1,0:T(8,128)S(1)} %get-tuple-element.20), channel_id=1, replica_groups=mesh['row'=16,'col'=2] {'row'}, dimensions={0}, use_global_device_ids=true | all-gather | bytes 208896 | tf_op jit(solution)/shard_map/all_gather | solution.py:78
  167.9 0.3 fusion.30
  168.2 22.6 %fusion.46 = (f32[48,384]{0,1:T(8,128)S(1)}, f32[48,384,128]{2,0,1:T(8,128)}) fusion(f32[128]{0:T(128)S(1)} %copy-done.8, f32[384,128]{1,0:T(8,128)S(1)} %fusion.30, f32[48,128]{1,0:T(8,128)S(1)} %fusion.32, f32[64,128]{1,0:T(8,128)S(1)} %slice-done.6, f32[384,64]{1,0:T(8,128)S(1)} %constant_dynamic-slice_fusion, f32[48,64]{1,0:T(8,128)S(1)} %get-tuple-element.21, ...), kind=kOutput, calls=%fused_computation.64 | convolution fusion | flops 1826863104 | bytes 19313152 | tf_op jit(solution)/shard_map/ip,jpc->ijc/dot_general | solution.py:87
  190.8 0.1 copy.57
  190.9 0.0 slice-start
  190.9 0.1 copy.58
  191.1 0.0 slice-start.1
  191.1 0.0 slice-start.2
  191.1 10.5 %copy.56 = f32[48,384,128]{2,1,0:T(8,128)} copy(f32[48,384,128]{2,0,1:T(8,128)} %get-tuple-element.41) | data formatting | bytes 18874368 | tf_op jit(solution)/shard_map/add | solution.py:92
  201.5 0.0 slice-done
  201.5 0.0 slice-done.2
  201.6 5.4 %multiply_reduce_fusion = f32[48,384]{0,1:T(8,128)S(1)} fusion(f32[48,384,128]{2,0,1:T(8,128)S(1)} %bitcast.65, f32[48,384]{0,1:T(8,128)S(1)} %copy.58), kind=kLoop, calls=%fused_computation.9 | loop fusion | flops 7059456 | bytes 9584640 | tf_op jit(solution)/shard_map/reduce_sum | solution.py:21
  207.0 0.1 copy.59
  207.1 0.0 copy-start.5
  207.2 0.0 slice-start.3
  207.2 11.4 %fusion.8 = f32[18432,128]{1,0:T(8,128)S(1)} fusion(f32[48,384,128]{2,1,0:T(8,128)} %copy.56, f32[18432]{0:T(1024)S(1)} %rsqrt.26, f32[18432]{0:T(1024)S(1)} %div.39), kind=kLoop, calls=%fused_computation.7 | loop fusion | flops 4718592 | bytes 19021824 | tf_op jit(solution)/shard_map/mul | solution.py:21
  218.6 0.0 copy-done.5
  218.6 0.0 slice-start.4
  218.6 0.0 slice-start.5
  218.6 0.0 copy-start.6
  218.6 33.8 %fusion.47 = f32[18432,512]{1,0:T(8,128)} fusion(f32[18432,128]{1,0:T(8,128)S(1)} %fusion.8, f32[128,512]{1,0:T(8,128)S(1)} %copy-done.5), kind=kOutput, calls=%fused_computation.65 | convolution fusion | flops 14495514624 | bytes 47448064 | tf_op jit(solution)/shard_map/dot_general | solution.py:94
  252.4 0.0 slice-done.5
  252.4 0.0 copy-done.6
  252.4 0.0 copy-start.1
  252.4 35.4 %fusion.2 = f32[18432,128]{1,0:T(8,128)} fusion(f32[18432,128]{1,0:T(8,128)S(1)} %bitcast.68, f32[512,128]{1,0:T(8,128)S(1)} %copy-done.6, f32[18432,512]{1,0:T(8,128)} %fusion.47), kind=kOutput, calls=%fused_computation.2 | convolution fusion | flops 14507311104 | bytes 56885248 | tf_op jit(solution)/shard_map/dot_general | solution.py:95
  (19 shorter events, 0.1 us)
Async XLA Ops:
  7.2 122.0 %copy-start = (f32[1024,512]{1,0:T(8,128)S(1)}, f32[1024,512]{1,0:T(8,128)}, u32[]{:S(2)}) copy-start(f32[1024,512]{1,0:T(8,128)} %param.19) | copy-start | bytes 6291460
  7.2 45.5 %all-gather.8.cloned.1.call-start = ((), (), s32[]{:S(2)}) async-start(), calls=%async_computation | async-start | bytes 1671168 | tf_op jit(solution)/shard_map/all_gather | solution.py:56
  7.9 85.3 %all-gather.10.cloned.1.call-start = ((), (), s32[]{:S(2)}) async-start(), calls=%async_computation.1 | async-start | bytes 1671168 | tf_op jit(solution)/shard_map/all_gather | solution.py:57
  15.6 14.0 %copy-start.7 = (f32[128,32]{0,1:T(8,128)S(1)}, f32[128,32]{0,1:T(8,128)}, u32[]{:S(2)}) copy-start(f32[128,32]{0,1:T(8,128)} %param.18) | copy-start | bytes 49156
  58.3 1.4 copy-start.2
  58.3 89.2 %copy-start.4 = (f32[128,128]{1,0:T(8,128)S(1)}, f32[128,128]{1,0:T(8,128)}, u32[]{:S(2)}) copy-start(f32[128,128]{1,0:T(8,128)} %param.22) | copy-start | bytes 196612
  58.3 109.8 %slice-start.6 = ((f32[128,128]{1,0:T(8,128)}), f32[64,128]{1,0:T(8,128)S(1)}, s32[]{:S(2)}) async-start(f32[128,128]{1,0:T(8,128)} %param.22), calls=%async_computation.8 | async-start | bytes 65536 | tf_op jit(solution)/shard_map/slice | solution.py:81
  108.7 59.4 %copy-start.8 = (f32[128]{0:T(128)S(1)}, f32[128]{0:T(128)}, u32[]{:S(2)}) copy-start(f32[128]{0:T(128)} %param.23) | copy-start | bytes 1540
  131.5 59.3 %copy-start.3 = (f32[48,512]{1,0:T(8,128)}, f32[48,512]{1,0:T(8,128)S(1)}, u32[]{:S(2)}) copy-start(f32[48,512]{1,0:T(8,128)S(1)} %get-tuple-element.39) | copy-start | bytes 294916
  190.9 10.6 %slice-start = ((s8[9437184]{0:T(1024)(128)(4,1)}), s8[1048576]{0:T(1024)(128)(4,1)S(1)}, s32[]{:S(2)}) async-start(s8[9437184]{0:T(1024)(128)(4,1)} %bitcast.64), calls=%async_computation.2 | async-start | bytes 2097152
  191.1 10.5 %slice-start.1 = ((s8[9437184]{0:T(1024)(128)(4,1)}), s8[4194304]{0:T(1024)(128)(4,1)S(1)}, s32[]{:S(2)}) async-start(s8[9437184]{0:T(1024)(128)(4,1)} %bitcast.64), calls=%async_computation.3 | async-start | bytes 8388608
  191.1 10.5 %slice-start.2 = ((s8[9437184]{0:T(1024)(128)(4,1)}), s8[4194304]{0:T(1024)(128)(4,1)S(1)}, s32[]{:S(2)}) async-start(s8[9437184]{0:T(1024)(128)(4,1)} %bitcast.64), calls=%async_computation.4 | async-start | bytes 8388608
  207.1 11.4 %copy-start.5 = (f32[128,512]{1,0:T(8,128)S(1)}, f32[128,512]{1,0:T(8,128)}, u32[]{:S(2)}) copy-start(f32[128,512]{1,0:T(8,128)} %param.24) | copy-start | bytes 786436
  207.2 45.3 %slice-start.3 = ((s8[9437184]{0:T(1024)(128)(4,1)}), s8[4194304]{0:T(1024)(128)(4,1)S(1)}, s32[]{:S(2)}) async-start(s8[9437184]{0:T(1024)(128)(4,1)} %bitcast.66), calls=%async_computation.5 | async-start | bytes 8388608
  218.6 33.8 %slice-start.4 = ((s8[9437184]{0:T(1024)(128)(4,1)}), s8[4194304]{0:T(1024)(128)(4,1)S(1)}, s32[]{:S(2)}) async-start(s8[9437184]{0:T(1024)(128)(4,1)} %bitcast.66), calls=%async_computation.6 | async-start | bytes 8388608
  218.6 33.8 %slice-start.5 = ((s8[9437184]{0:T(1024)(128)(4,1)}), s8[1048576]{0:T(1024)(128)(4,1)S(1)}, s32[]{:S(2)}) async-start(s8[9437184]{0:T(1024)(128)(4,1)} %bitcast.66), calls=%async_computation.7 | async-start | bytes 2097152
  218.6 33.8 %copy-start.6 = (f32[512,128]{1,0:T(8,128)S(1)}, f32[512,128]{1,0:T(8,128)}, u32[]{:S(2)}) copy-start(f32[512,128]{1,0:T(8,128)} %param.25) | copy-start | bytes 786436
  252.4 35.5 %copy-start.1 = (f32[1024,512]{1,0:T(8,128)S(1)}, f32[1024,512]{1,0:T(8,128)}, u32[]{:S(2)}) copy-start(f32[1024,512]{1,0:T(8,128)} %param.19) | copy-start | bytes 6291460
Sparse Core Ops, SparseCore 0:
  10.3 42.3 all-gather.7
  54.9 38.2 all-gather.9
where the time goes:
time: 298 us; the launch traced here: 295 us
  matrix products  124 us (42%)
  blocking collectives  67.2 us (23%)
  waiting for transfers between devices  41.3 us (14%)
  other arithmetic  33.6 us (11%)
  between operations  14.6 us (5%)
  local copies, waits for them, and re-layouts  14.4 us (5%)
    dot_general x1, matrix products, per_device(): pair_new = flat + jnp.dot(hidden_act, w_down, precision=HIGH)  35.4 us
    dot_general x1, matrix products, per_device(): hidden_act = jax.nn.relu(jnp.dot(channel_norm(flat), w_up, precision=HIGH))  33.8 us
    all_gather x1, waiting for transfers between devices, per_device(): lax.all_gather(value, 'row', axis=1, tiled=True)  32.7 us
    all_gather x3, blocking collectives, merged(): everything = jax.tree.map(lambda part: lax.all_gather(part, axis), x)  26.8 us
    dot_general x1, matrix products, per_device(): jnp.einsum('ip,jpc->ijc', left, table, precision=HIGH)  22.6 us
    all_gather x1, blocking collectives, per_device(): right_every = lax.all_gather(right, 'row', axis=0, tiled=True)  20.2 us
    dot_general x1, matrix products, per_device(): bias = jnp.einsum('ijc,ch->ihj', channel_norm(pair), w_bias, precision=HIGH)  15.9 us
    reduce_sum x2, other arithmetic, channel_norm(): jnp.mean(centre * centre, axis=-1, keepdims=True) + 1e-05  13.1 us
  transfers between devices with their start and end apart: 2, of which 2 were waited for; matrix products, arithmetic and copies ran while one was open for 12% of the time, Pallas kernels for 0%

commit v1 on v0

--- a/solution.py
+++ b/solution.py
@@ -4,6 +4,16 @@
 from jax.sharding import PartitionSpec as P
 
 HIGH = lax.Precision.HIGHEST
+
+
+def ring_gather(x, axis, dim):
+    ways, here, turn = (lax.axis_size(axis), lax.axis_index(axis), x.shape[dim])
+    shape = [n * ways if d == dim else n for d, n in enumerate(x.shape)]
+    full = lax.dynamic_update_slice_in_dim(jnp.zeros(shape, x.dtype), x, here * turn, axis=dim)
+    for far in range(1, ways):
+        x = lax.ppermute(x, axis, [(d, (d + 1) % ways) for d in range(ways)])
+        full = lax.dynamic_update_slice_in_dim(full, x, (here - far) % ways * turn, axis=dim)
+    return full
 
 
 def merged(x, axis, combine):
@@ -54,7 +64,7 @@
     queries = lax.all_gather(query, "col", axis=1, tiled=True)
     keys_all, values_all = (
         lax.all_gather(key, "row", axis=1, tiled=True),
-        lax.all_gather(value, "row", axis=1, tiled=True),
+        ring_gather(value, "row", 1),
     )
     parts = partial_softmax(
         queries.reshape(rows_here, heads, head_dim),

time: 298 us -> 346 us (1.16)
  waiting for transfers between devices: 41.3 us -> 85.4 us
  local copies, waits for them, and re-layouts: 14.4 us -> 24 us
  blocking collectives: 67.2 us -> 61.3 us
    ppermute x0 -> x15, waiting for transfers between devices: none -> 84.7 us  [ring_gather(): x = lax.ppermute(x, axis, [(d, (d + 1) % ways) for d in range(ways)])]
    all_gather x1 -> x0, waiting for transfers between devices: 32.7 us -> none  [per_device(): lax.all_gather(value, 'row', axis=1, tiled=True)]
    dynamic_update_slice x0 -> x16, local copies, waits for them, and re-layouts: none -> 10.3 us  [the longest x15 9.65 us: ring_gather(): lax.dynamic_update_slice_in_dim(full, x, (here - far) % ways * turn, axis...]
    all_gather x1, waiting for transfers between devices: 7.2 us -> 0.01 us  [per_device(): lax.all_gather(key, 'row', axis=1, tiled=True)]
    all_gather x3, blocking collectives: 26.8 us -> 22.2 us  [merged(): everything = jax.tree.map(lambda part: lax.all_gather(part, axis), x)]
  transfers between devices with their start and end apart: 2 -> 16, of which waited for: 2 -> 14; matrix products, arithmetic and copies ran while one was open for 12% -> 12% of each run, Pallas kernels for 0% -> 0%
where the time goes in v1:
time: 346 us; the launch traced here: 340 us
  matrix products  121 us (35%)
  waiting for transfers between devices  85.4 us (25%)
  blocking collectives  61.3 us (18%)
  other arithmetic  32.1 us (9%)
  local copies, waits for them, and re-layouts  24 us (7%)
  between operations  14.8 us (4%)
    ppermute x15, waiting for transfers between devices, ring_gather(): x = lax.ppermute(x, axis, [(d, (d + 1) % ways) for d in range(ways)])  84.7 us
    dot_general x1, matrix products, per_device(): pair_new = flat + jnp.dot(hidden_act, w_down, precision=HIGH)  35.4 us
    dot_general x1, matrix products, per_device(): hidden_act = jax.nn.relu(jnp.dot(channel_norm(flat), w_up, precision=HIGH))  33.8 us
    dot_general x1, matrix products, per_device(): jnp.einsum('ip,jpc->ijc', left, table, precision=HIGH)  22.6 us
    all_gather x3, blocking collectives, merged(): everything = jax.tree.map(lambda part: lax.all_gather(part, axis), x)  22.2 us
    all_gather x1, blocking collectives, per_device(): right_every = lax.all_gather(right, 'row', axis=0, tiled=True)  18.8 us
    dot_general x1, matrix products, per_device(): bias = jnp.einsum('ijc,ch->ihj', channel_norm(pair), w_bias, precision=HIGH)  15.9 us
    reduce_sum x2, other arithmetic, channel_norm(): jnp.mean(centre * centre, axis=-1, keepdims=True) + 1e-05  12.9 us
  transfers between devices with their start and end apart: 16, of which 14 were waited for; matrix products, arithmetic and copies ran while one was open for 12% of the time, Pallas kernels for 0%

profile of v1, /device:TPU:0, one launch (start us, length us, event | category | flops | bytes accessed | tf_op | source)
XLA Modules:
  0.0 340.3 jit_solution(10046917571931203702)
XLA Ops:
  7.2 0.7 all-gather.7.cloned.1.call-update
  7.9 0.5 collective-permute-start
  8.5 6.2 %reduce_sum.63 = f32[48,384]{1,0:T(8,128)S(1)} reduce(f32[48,384,128]{2,1,0:T(8,128)} %param.17, f32[]{:T(128)} %constant.133.clone.1), dimensions={2}, to_apply=%region_0.0 | reduce | flops 2340864 | bytes 9510916 | tf_op jit(solution)/shard_map/reduce_sum | solution.py:30
  14.7 6.4 %all_gather.28 = f32[48,1024]{1,0:T(8,128)S(1)} all-gather(f32[48,512]{1,0:T(8,128)S(1)} %copy-done.9), channel_id=1, replica_groups=mesh['row'=16,'col'=2] {'col'}, dimensions={1}, use_global_device_ids=true | all-gather | bytes 294912 | tf_op jit(solution)/shard_map/all_gather | solution.py:64
  21.1 0.2 copy.49
  21.4 7.4 %multiply_reduce_fusion.1 = f32[48,384]{1,0:T(8,128)S(1)} fusion(f32[48,384,128]{2,1,0:T(8,128)} %param.17, f32[48,384]{1,0:T(8,128)S(1)} %broadcast_multiply_fusion.1), kind=kLoop, calls=%fused_computation.12 | loop fusion | flops 7059456 | bytes 9584640 | tf_op jit(solution)/shard_map/reduce_sum | solution.py:31
  28.9 15.9 %fusion.9 = f32[48,384,32]{1,2,0:T(8,128)} fusion(f32[48,384,128]{2,1,0:T(8,128)} %param.17, f32[48,384]{1,0:T(8,128)S(1)} %add_rsqrt_fusion.1, f32[48,384]{1,0:T(8,128)S(1)} %broadcast_multiply_fusion.1, f32[128,32]{0,1:T(8,128)S(1)} %copy-done.10), kind=kOutput, calls=%fused_computation.10 | convolution fusion | flops 910688256 | bytes 11960320 | tf_op jit(solution)/shard_map/ijc,ch->ihj/dot_general | solution.py:63
  44.8 1.2 broadcast_in_dim.4
  46.0 0.6 constant_dynamic-update-slice_fusion.15
  46.7 0.6 collective-permute-start.1
  47.3 0.6 constant_dynamic-update-slice_fusion.14
  47.9 5.5 %collective-permute-done.1 = f32[384,64]{0,1:T(8,128)S(1)} collective-permute-done((f32[384,64]{0,1:T(8,128)S(1)}, f32[384,64]{0,1:T(8,128)S(1)}, u32[]{:S(2)}, u32[]{:S(2)}) %collective-permute-start.1) | collective-permute-done | bytes 98336 | tf_op jit(solution)/shard_map/ppermute | solution.py:14
  53.4 0.6 constant_dynamic-update-slice_fusion.13
  54.1 6.1 %collective-permute-done.2 = f32[384,64]{0,1:T(8,128)S(1)} collective-permute-done((f32[384,64]{0,1:T(8,128)S(1)}, f32[384,64]{0,1:T(8,128)S(1)}, u32[]{:S(2)}, u32[]{:S(2)}) %collective-permute-start.2) | collective-permute-done | bytes 98336 | tf_op jit(solution)/shard_map/ppermute | solution.py:14
  60.2 0.6 constant_dynamic-update-slice_fusion.12
  60.8 6.1 %collective-permute-done.3 = f32[384,64]{0,1:T(8,128)S(1)} collective-permute-done((f32[384,64]{0,1:T(8,128)S(1)}, f32[384,64]{0,1:T(8,128)S(1)}, u32[]{:S(2)}, u32[]{:S(2)}) %collective-permute-start.3) | collective-permute-done | bytes 98336 | tf_op jit(solution)/shard_map/ppermute | solution.py:14
  66.9 0.6 constant_dynamic-update-slice_fusion.11
  67.5 6.1 %collective-permute-done.4 = f32[384,64]{0,1:T(8,128)S(1)} collective-permute-done((f32[384,64]{0,1:T(8,128)S(1)}, f32[384,64]{0,1:T(8,128)S(1)}, u32[]{:S(2)}, u32[]{:S(2)}) %collective-permute-start.4) | collective-permute-done | bytes 98336 | tf_op jit(solution)/shard_map/ppermute | solution.py:14
  73.6 0.6 constant_dynamic-update-slice_fusion.10
  74.3 6.1 %collective-permute-done.5 = f32[384,64]{0,1:T(8,128)S(1)} collective-permute-done((f32[384,64]{0,1:T(8,128)S(1)}, f32[384,64]{0,1:T(8,128)S(1)}, u32[]{:S(2)}, u32[]{:S(2)}) %collective-permute-start.5) | collective-permute-done | bytes 98336 | tf_op jit(solution)/shard_map/ppermute | solution.py:14
  80.4 0.6 constant_dynamic-update-slice_fusion.9
  81.0 6.1 %collective-permute-done.6 = f32[384,64]{0,1:T(8,128)S(1)} collective-permute-done((f32[384,64]{0,1:T(8,128)S(1)}, f32[384,64]{0,1:T(8,128)S(1)}, u32[]{:S(2)}, u32[]{:S(2)}) %collective-permute-start.6) | collective-permute-done | bytes 98336 | tf_op jit(solution)/shard_map/ppermute | solution.py:14
  87.1 0.7 constant_dynamic-update-slice_fusion.8
  87.8 6.1 %collective-permute-done.7 = f32[384,64]{0,1:T(8,128)S(1)} collective-permute-done((f32[384,64]{0,1:T(8,128)S(1)}, f32[384,64]{0,1:T(8,128)S(1)}, u32[]{:S(2)}, u32[]{:S(2)}) %collective-permute-start.7) | collective-permute-done | bytes 98336 | tf_op jit(solution)/shard_map/ppermute | solution.py:14
  93.9 0.6 constant_dynamic-update-slice_fusion.7
  94.5 6.1 %collective-permute-done.8 = f32[384,64]{0,1:T(8,128)S(1)} collective-permute-done((f32[384,64]{0,1:T(8,128)S(1)}, f32[384,64]{0,1:T(8,128)S(1)}, u32[]{:S(2)}, u32[]{:S(2)}) %collective-permute-start.8) | collective-permute-done | bytes 98336 | tf_op jit(solution)/shard_map/ppermute | solution.py:14
  100.6 0.6 constant_dynamic-update-slice_fusion.6
  101.2 6.1 %collective-permute-done.9 = f32[384,64]{0,1:T(8,128)S(1)} collective-permute-done((f32[384,64]{0,1:T(8,128)S(1)}, f32[384,64]{0,1:T(8,128)S(1)}, u32[]{:S(2)}, u32[]{:S(2)}) %collective-permute-start.9) | collective-permute-done | bytes 98336 | tf_op jit(solution)/shard_map/ppermute | solution.py:14
  107.3 0.7 constant_dynamic-update-slice_fusion.5
  108.0 6.1 %collective-permute-done.10 = f32[384,64]{0,1:T(8,128)S(1)} collective-permute-done((f32[384,64]{0,1:T(8,128)S(1)}, f32[384,64]{0,1:T(8,128)S(1)}, u32[]{:S(2)}, u32[]{:S(2)}) %collective-permute-start.10) | collective-permute-done | bytes 98336 | tf_op jit(solution)/shard_map/ppermute | solution.py:14
  114.1 0.6 constant_dynamic-update-slice_fusion.4
  114.7 6.1 %collective-permute-done.11 = f32[384,64]{0,1:T(8,128)S(1)} collective-permute-done((f32[384,64]{0,1:T(8,128)S(1)}, f32[384,64]{0,1:T(8,128)S(1)}, u32[]{:S(2)}, u32[]{:S(2)}) %collective-permute-start.11) | collective-permute-done | bytes 98336 | tf_op jit(solution)/shard_map/ppermute | solution.py:14
  120.8 0.6 constant_dynamic-update-slice_fusion.3
  121.5 6.1 %collective-permute-done.12 = f32[384,64]{0,1:T(8,128)S(1)} collective-permute-done((f32[384,64]{0,1:T(8,128)S(1)}, f32[384,64]{0,1:T(8,128)S(1)}, u32[]{:S(2)}, u32[]{:S(2)}) %collective-permute-start.12) | collective-permute-done | bytes 98336 | tf_op jit(solution)/shard_map/ppermute | solution.py:14
  127.6 0.6 constant_dynamic-update-slice_fusion.2
  128.2 6.1 %collective-permute-done.13 = f32[384,64]{0,1:T(8,128)S(1)} collective-permute-done((f32[384,64]{0,1:T(8,128)S(1)}, f32[384,64]{0,1:T(8,128)S(1)}, u32[]{:S(2)}, u32[]{:S(2)}) %collective-permute-start.13) | collective-permute-done | bytes 98336 | tf_op jit(solution)/shard_map/ppermute | solution.py:14
  134.3 0.3 collective-permute-start.14
  134.6 0.7 constant_dynamic-update-slice_fusion.1
  135.2 6.1 %collective-permute-done.14 = f32[384,64]{0,1:T(8,128)S(1)} collective-permute-done((f32[384,64]{0,1:T(8,128)S(1)}, f32[384,64]{0,1:T(8,128)S(1)}, u32[]{:S(2)}, u32[]{:S(2)}) %collective-permute-start.14) | collective-permute-done | bytes 98336 | tf_op jit(solution)/shard_map/ppermute | solution.py:14
  141.3 0.6 constant_dynamic-update-slice_fusion
  141.9 5.7 %fusion.45 = (f32[48,32]{0,1:T(8,128)S(1)}, f32[48,32,384]{2,0,1:T(8,128)S(1)}) fusion(f32[48,384,32]{1,2,0:T(8,128)} %fusion.9, f32[384,32,32]{0,2,1:T(8,128)} %bitcast.71, f32[48,32,32]{0,2,1:T(8,128)S(1)} %bitcast.70), kind=kOutput, calls=%fused_computation.79 | convolution fusion | flops 228260352 | bytes 6494208 | tf_op jit(solution)/shard_map/ihd,jhd->ihj/dot_general | solution.py:44
  147.6 0.8 fusion.18
  148.4 4.3 %fusion.20 = f32[48,32,32]{0,2,1:T(8,128)S(1)} fusion(f32[384,32,32]{0,2,1:T(8,128)} %bitcast, f32[48,32,384]{2,0,1:T(8,128)S(1)} %get-tuple-element.38, f32[48,32]{0,1:T(8,128)S(1)} %get-tuple-element.37), kind=kOutput, calls=%fused_computation.22 | convolution fusion | flops 227082240 | bytes 4134912 | tf_op jit(solution)/shard_map/ihj,jhd->ihd/dot_general | solution.py:48
  152.8 4.8 %all-gather.3 = f32[2,48,32]{1,2,0:T(8,128)S(1)} all-gather(f32[1,48,32]{1,2,0:T(8,128)S(1)} %bitcast.72), channel_id=3, replica_groups=mesh['row'=16,'col'=2] {'col'}, dimensions={0}, use_global_device_ids=true | all-gather | bytes 18432 | tf_op jit(solution)/shard_map/all_gather | solution.py:20
  157.6 4.6 %all-gather.4 = f32[2,48,32]{1,2,0:T(8,128)S(1)} all-gather(f32[1,48,32]{1,2,0:T(8,128)S(1)} %bitcast.73), channel_id=4, replica_groups=mesh['row'=16,'col'=2] {'col'}, dimensions={0}, use_global_device_ids=true | all-gather | bytes 18432 | tf_op jit(solution)/shard_map/all_gather | solution.py:20
  162.4 0.7 copy.51
  163.2 12.8 %all-gather = f32[96,32,32]{2,1,0:T(8,128)S(1)} all-gather(f32[48,32,32]{2,1,0:T(8,128)S(1)} %copy.51), channel_id=2, replica_groups=mesh['row'=16,'col'=2] {'col'}, dimensions={0}, use_global_device_ids=true | all-gather | bytes 589824 | tf_op jit(solution)/shard_map/all_gather | solution.py:20
  175.9 0.8 fusion.23
  176.7 0.4 reshape.150
  177.1 2.4 fusion.42
  179.5 4.9 %all-reduce.1 = (f32[48]{0:T(128)S(1)}, f32[48]{0:T(128)S(1)}) all-reduce(f32[48]{0:T(128)S(1)} %get-tuple-element.19, f32[48]{0:T(128)S(1)} %get-tuple-element.18), channel_id=1, replica_groups=mesh['row'=16,'col'=2] {'col'}, use_global_device_ids=true, to_apply=%region_7.8 | all-reduce | flops 96 | bytes 768 | tf_op jit(solution)/shard_map/psum | solution.py:79
  184.4 0.3 fusion.24
  184.7 0.3 fusion.25
  185.1 9.1 %all-reduce = (f32[48,64]{1,0:T(8,128)S(1)}, f32[48,64]{1,0:T(8,128)S(1)}) all-reduce(f32[48,64]{1,0:T(8,128)S(1)} %fusion.24, f32[48,64]{1,0:T(8,128)S(1)} %fusion.25), channel_id=1, replica_groups=mesh['row'=16,'col'=2] {'col'}, use_global_device_ids=true, to_apply=%region_9.10 | all-reduce | flops 6144 | bytes 49152 | tf_op jit(solution)/shard_map/psum | solution.py:87
  194.2 0.2 fusion.32
  194.3 18.8 %all_gather.35 = f32[768,64]{1,0:T(8,128)S(1)} all-gather(f32[48,64]{1,0:T(8,128)S(1)} %get-tuple-element.20), channel_id=1, replica_groups=mesh['row'=16,'col'=2] {'row'}, dimensions={0}, use_global_device_ids=true | all-gather | bytes 208896 | tf_op jit(solution)/shard_map/all_gather | solution.py:88
  213.1 0.3 fusion.30
  213.5 22.6 %fusion.46 = (f32[48,384]{0,1:T(8,128)S(1)}, f32[48,384,128]{2,0,1:T(8,128)}) fusion(f32[128]{0:T(128)S(1)} %copy-done.11, f32[384,128]{1,0:T(8,128)S(1)} %fusion.30, f32[48,128]{1,0:T(8,128)S(1)} %fusion.32, f32[64,128]{1,0:T(8,128)S(1)} %slice-done.6, f32[384,64]{1,0:T(8,128)S(1)} %constant_dynamic-slice_fusion, f32[48,64]{1,0:T(8,128)S(1)} %get-tuple-element.21, ...), kind=kOutput, calls=%fused_computation.80 | convolution fusion | flops 1826863104 | bytes 19313152 | tf_op jit(solution)/shard_map/ip,jpc->ijc/dot_general | solution.py:97
  236.2 0.1 copy.58
  236.3 10.5 %copy.56 = f32[48,384,128]{2,1,0:T(8,128)} copy(f32[48,384,128]{2,0,1:T(8,128)} %get-tuple-element.41) | data formatting | bytes 18874368 | tf_op jit(solution)/shard_map/add | solution.py:102
  246.9 5.4 %multiply_reduce_fusion = f32[48,384]{0,1:T(8,128)S(1)} fusion(f32[48,384,128]{2,0,1:T(8,128)S(1)} %bitcast.65, f32[48,384]{0,1:T(8,128)S(1)} %copy.58), kind=kLoop, calls=%fused_computation.9 | loop fusion | flops 7059456 | bytes 9584640 | tf_op jit(solution)/shard_map/reduce_sum | solution.py:31
  252.5 11.4 %fusion.8 = f32[18432,128]{1,0:T(8,128)S(1)} fusion(f32[48,384,128]{2,1,0:T(8,128)} %copy.56, f32[18432]{0:T(1024)S(1)} %rsqrt.26, f32[18432]{0:T(1024)S(1)} %div.39), kind=kLoop, calls=%fused_computation.7 | loop fusion | flops 4718592 | bytes 19021824 | tf_op jit(solution)/shard_map/mul | solution.py:31
  263.9 33.8 %fusion.47 = f32[18432,512]{1,0:T(8,128)} fusion(f32[18432,128]{1,0:T(8,128)S(1)} %fusion.8, f32[128,512]{1,0:T(8,128)S(1)} %copy-done.4), kind=kOutput, calls=%fused_computation.81 | convolution fusion | flops 14495514624 | bytes 47448064 | tf_op jit(solution)/shard_map/dot_general | solution.py:104
  297.8 35.4 %fusion.2 = f32[18432,128]{1,0:T(8,128)} fusion(f32[18432,128]{1,0:T(8,128)S(1)} %bitcast.68, f32[512,128]{1,0:T(8,128)S(1)} %copy-done.5, f32[18432,512]{1,0:T(8,128)} %fusion.47), kind=kOutput, calls=%fused_computation.2 | convolution fusion | flops 14507311104 | bytes 56885248 | tf_op jit(solution)/shard_map/dot_general | solution.py:105
  (69 shorter events, 0.7 us)
Async XLA Ops:
  7.2 169.9 %copy-start = (f32[1024,512]{1,0:T(8,128)S(1)}, f32[1024,512]{1,0:T(8,128)}, u32[]{:S(2)}) copy-start(f32[1024,512]{1,0:T(8,128)} %param.19) | copy-start | bytes 6291460
  7.2 134.8 %all-gather.7.cloned.1.call-start = ((), (), s32[]{:S(2)}) async-start(), calls=%async_computation | async-start | bytes 1671168 | tf_op jit(solution)/shard_map/all_gather | solution.py:66
  7.9 38.8 %collective-permute-start = (f32[384,64]{0,1:T(8,128)}, f32[384,64]{0,1:T(8,128)S(1)}, u32[]{:S(2)}, u32[]{:S(2)}) collective-permute-start(f32[384,64]{0,1:T(8,128)} %param.16), channel_id=1, source_target_pairs={{0,2},{2,4},{4,6},{6,8},{8,10},{10,12},{12,14},{14,16},{16,18},{18... | collective-permute-start | bytes 294920 | tf_op jit(solution)/shard_map/ppermute | solution.py:14
  8.5 6.2 %copy-start.9 = (f32[48,512]{1,0:T(8,128)S(1)}, f32[48,512]{1,0:T(8,128)}, u32[]{:S(2)}) copy-start(f32[48,512]{1,0:T(8,128)} %param.14) | copy-start | bytes 294916
  21.4 7.5 %copy-start.10 = (f32[128,32]{0,1:T(8,128)S(1)}, f32[128,32]{0,1:T(8,128)}, u32[]{:S(2)}) copy-start(f32[128,32]{0,1:T(8,128)} %param.18) | copy-start | bytes 49156
  28.8 17.2 %copy-start.8 = (f32[384,64]{0,1:T(8,128)S(1)}, f32[384,64]{0,1:T(8,128)}, u32[]{:S(2)}) copy-start(f32[384,64]{0,1:T(8,128)} %param.16) | copy-start | bytes 294916
  46.7 6.7 %collective-permute-start.1 = (f32[384,64]{0,1:T(8,128)S(1)}, f32[384,64]{0,1:T(8,128)S(1)}, u32[]{:S(2)}, u32[]{:S(2)}) collective-permute-start(f32[384,64]{0,1:T(8,128)S(1)} %collective-permute-done), channel_id=1, source_target_pairs={{0,2},{2,4},{4,6},{6,8},{8,10},{10,12},{12,14},{14,16},{16,18},{18... | collective-permute-start | bytes 294920 | tf_op jit(solution)/shard_map/ppermute | solution.py:14
  53.4 6.7 %collective-permute-start.2 = (f32[384,64]{0,1:T(8,128)S(1)}, f32[384,64]{0,1:T(8,128)S(1)}, u32[]{:S(2)}, u32[]{:S(2)}) collective-permute-start(f32[384,64]{0,1:T(8,128)S(1)} %collective-permute-done.1), channel_id=1, source_target_pairs={{0,2},{2,4},{4,6},{6,8},{8,10},{10,12},{12,14},{14,16},{16,18},{18... | collective-permute-start | bytes 294920 | tf_op jit(solution)/shard_map/ppermute | solution.py:14
  60.2 6.7 %collective-permute-start.3 = (f32[384,64]{0,1:T(8,128)S(1)}, f32[384,64]{0,1:T(8,128)S(1)}, u32[]{:S(2)}, u32[]{:S(2)}) collective-permute-start(f32[384,64]{0,1:T(8,128)S(1)} %collective-permute-done.2), channel_id=1, source_target_pairs={{0,2},{2,4},{4,6},{6,8},{8,10},{10,12},{12,14},{14,16},{16,18},{18... | collective-permute-start | bytes 294920 | tf_op jit(solution)/shard_map/ppermute | solution.py:14
  66.9 6.7 %collective-permute-start.4 = (f32[384,64]{0,1:T(8,128)S(1)}, f32[384,64]{0,1:T(8,128)S(1)}, u32[]{:S(2)}, u32[]{:S(2)}) collective-permute-start(f32[384,64]{0,1:T(8,128)S(1)} %collective-permute-done.3), channel_id=1, source_target_pairs={{0,2},{2,4},{4,6},{6,8},{8,10},{10,12},{12,14},{14,16},{16,18},{18... | collective-permute-start | bytes 294920 | tf_op jit(solution)/shard_map/ppermute | solution.py:14
  73.6 6.7 %collective-permute-start.5 = (f32[384,64]{0,1:T(8,128)S(1)}, f32[384,64]{0,1:T(8,128)S(1)}, u32[]{:S(2)}, u32[]{:S(2)}) collective-permute-start(f32[384,64]{0,1:T(8,128)S(1)} %collective-permute-done.4), channel_id=1, source_target_pairs={{0,2},{2,4},{4,6},{6,8},{8,10},{10,12},{12,14},{14,16},{16,18},{18... | collective-permute-start | bytes 294920 | tf_op jit(solution)/shard_map/ppermute | solution.py:14
  80.4 6.7 %collective-permute-start.6 = (f32[384,64]{0,1:T(8,128)S(1)}, f32[384,64]{0,1:T(8,128)S(1)}, u32[]{:S(2)}, u32[]{:S(2)}) collective-permute-start(f32[384,64]{0,1:T(8,128)S(1)} %collective-permute-done.5), channel_id=1, source_target_pairs={{0,2},{2,4},{4,6},{6,8},{8,10},{10,12},{12,14},{14,16},{16,18},{18... | collective-permute-start | bytes 294920 | tf_op jit(solution)/shard_map/ppermute | solution.py:14
  87.1 6.7 %collective-permute-start.7 = (f32[384,64]{0,1:T(8,128)S(1)}, f32[384,64]{0,1:T(8,128)S(1)}, u32[]{:S(2)}, u32[]{:S(2)}) collective-permute-start(f32[384,64]{0,1:T(8,128)S(1)} %collective-permute-done.6), channel_id=1, source_target_pairs={{0,2},{2,4},{4,6},{6,8},{8,10},{10,12},{12,14},{14,16},{16,18},{18... | collective-permute-start | bytes 294920 | tf_op jit(solution)/shard_map/ppermute | solution.py:14
  93.9 6.7 %collective-permute-start.8 = (f32[384,64]{0,1:T(8,128)S(1)}, f32[384,64]{0,1:T(8,128)S(1)}, u32[]{:S(2)}, u32[]{:S(2)}) collective-permute-start(f32[384,64]{0,1:T(8,128)S(1)} %collective-permute-done.7), channel_id=1, source_target_pairs={{0,2},{2,4},{4,6},{6,8},{8,10},{10,12},{12,14},{14,16},{16,18},{18... | collective-permute-start | bytes 294920 | tf_op jit(solution)/shard_map/ppermute | solution.py:14
  100.6 6.7 %collective-permute-start.9 = (f32[384,64]{0,1:T(8,128)S(1)}, f32[384,64]{0,1:T(8,128)S(1)}, u32[]{:S(2)}, u32[]{:S(2)}) collective-permute-start(f32[384,64]{0,1:T(8,128)S(1)} %collective-permute-done.8), channel_id=1, source_target_pairs={{0,2},{2,4},{4,6},{6,8},{8,10},{10,12},{12,14},{14,16},{16,18},{18... | collective-permute-start | bytes 294920 | tf_op jit(solution)/shard_map/ppermute | solution.py:14
  107.3 6.7 %collective-permute-start.10 = (f32[384,64]{0,1:T(8,128)S(1)}, f32[384,64]{0,1:T(8,128)S(1)}, u32[]{:S(2)}, u32[]{:S(2)}) collective-permute-start(f32[384,64]{0,1:T(8,128)S(1)} %collective-permute-done.9), channel_id=1, source_target_pairs={{0,2},{2,4},{4,6},{6,8},{8,10},{10,12},{12,14},{14,16},{16,18},{18... | collective-permute-start | bytes 294920 | tf_op jit(solution)/shard_map/ppermute | solution.py:14
  114.1 6.7 %collective-permute-start.11 = (f32[384,64]{0,1:T(8,128)S(1)}, f32[384,64]{0,1:T(8,128)S(1)}, u32[]{:S(2)}, u32[]{:S(2)}) collective-permute-start(f32[384,64]{0,1:T(8,128)S(1)} %collective-permute-done.10), channel_id=1, source_target_pairs={{0,2},{2,4},{4,6},{6,8},{8,10},{10,12},{12,14},{14,16},{16,18},{18... | collective-permute-start | bytes 294920 | tf_op jit(solution)/shard_map/ppermute | solution.py:14
  120.8 6.7 %collective-permute-start.12 = (f32[384,64]{0,1:T(8,128)S(1)}, f32[384,64]{0,1:T(8,128)S(1)}, u32[]{:S(2)}, u32[]{:S(2)}) collective-permute-start(f32[384,64]{0,1:T(8,128)S(1)} %collective-permute-done.11), channel_id=1, source_target_pairs={{0,2},{2,4},{4,6},{6,8},{8,10},{10,12},{12,14},{14,16},{16,18},{18... | collective-permute-start | bytes 294920 | tf_op jit(solution)/shard_map/ppermute | solution.py:14
  127.6 6.7 %collective-permute-start.13 = (f32[384,64]{0,1:T(8,128)S(1)}, f32[384,64]{0,1:T(8,128)S(1)}, u32[]{:S(2)}, u32[]{:S(2)}) collective-permute-start(f32[384,64]{0,1:T(8,128)S(1)} %collective-permute-done.12), channel_id=1, source_target_pairs={{0,2},{2,4},{4,6},{6,8},{8,10},{10,12},{12,14},{14,16},{16,18},{18... | collective-permute-start | bytes 294920 | tf_op jit(solution)/shard_map/ppermute | solution.py:14
  134.3 7.0 %collective-permute-start.14 = (f32[384,64]{0,1:T(8,128)S(1)}, f32[384,64]{0,1:T(8,128)S(1)}, u32[]{:S(2)}, u32[]{:S(2)}) collective-permute-start(f32[384,64]{0,1:T(8,128)S(1)} %collective-permute-done.13), channel_id=1, source_target_pairs={{0,2},{2,4},{4,6},{6,8},{8,10},{10,12},{12,14},{14,16},{16,18},{18... | collective-permute-start | bytes 294920 | tf_op jit(solution)/shard_map/ppermute | solution.py:14
  175.9 8.5 %copy-start.6 = (f32[512,64]{0,1:T(8,128)S(1)}, f32[512,64]{0,1:T(8,128)}, u32[]{:S(2)}) copy-start(f32[512,64]{0,1:T(8,128)} %param.21) | copy-start | bytes 393220
  176.7 8.1 %copy-start.7 = (f32[512,64]{0,1:T(8,128)S(1)}, f32[512,64]{0,1:T(8,128)}, u32[]{:S(2)}) copy-start(f32[512,64]{0,1:T(8,128)} %param.20) | copy-start | bytes 393220
  176.7 17.5 %copy-start.3 = (f32[128,128]{1,0:T(8,128)S(1)}, f32[128,128]{1,0:T(8,128)}, u32[]{:S(2)}) copy-start(f32[128,128]{1,0:T(8,128)} %param.22) | copy-start | bytes 196612
  177.1 36.4 %slice-start.6 = ((f32[128,128]{1,0:T(8,128)}), f32[64,128]{1,0:T(8,128)S(1)}, s32[]{:S(2)}) async-start(f32[128,128]{1,0:T(8,128)} %param.22), calls=%async_computation.7 | async-start | bytes 65536 | tf_op jit(solution)/shard_map/slice | solution.py:91
  177.1 36.3 %copy-start.11 = (f32[128]{0:T(128)S(1)}, f32[128]{0:T(128)}, u32[]{:S(2)}) copy-start(f32[128]{0:T(128)} %param.23) | copy-start | bytes 1540
  179.5 56.6 %copy-start.2 = (f32[48,512]{1,0:T(8,128)}, f32[48,512]{1,0:T(8,128)S(1)}, u32[]{:S(2)}) copy-start(f32[48,512]{1,0:T(8,128)S(1)} %get-tuple-element.39) | copy-start | bytes 294916
  236.2 10.7 %slice-start = ((s8[9437184]{0:T(1024)(128)(4,1)}), s8[1048576]{0:T(1024)(128)(4,1)S(1)}, s32[]{:S(2)}) async-start(s8[9437184]{0:T(1024)(128)(4,1)} %bitcast.64), calls=%async_computation.1 | async-start | bytes 2097152
  236.3 10.5 %slice-start.1 = ((s8[9437184]{0:T(1024)(128)(4,1)}), s8[4194304]{0:T(1024)(128)(4,1)S(1)}, s32[]{:S(2)}) async-start(s8[9437184]{0:T(1024)(128)(4,1)} %bitcast.64), calls=%async_computation.2 | async-start | bytes 8388608
  236.3 10.5 %slice-start.2 = ((s8[9437184]{0:T(1024)(128)(4,1)}), s8[4194304]{0:T(1024)(128)(4,1)S(1)}, s32[]{:S(2)}) async-start(s8[9437184]{0:T(1024)(128)(4,1)} %bitcast.64), calls=%async_computation.3 | async-start | bytes 8388608
  252.5 11.4 %copy-start.4 = (f32[128,512]{1,0:T(8,128)S(1)}, f32[128,512]{1,0:T(8,128)}, u32[]{:S(2)}) copy-start(f32[128,512]{1,0:T(8,128)} %param.24) | copy-start | bytes 786436
  252.5 45.3 %slice-start.3 = ((s8[9437184]{0:T(1024)(128)(4,1)}), s8[4194304]{0:T(1024)(128)(4,1)S(1)}, s32[]{:S(2)}) async-start(s8[9437184]{0:T(1024)(128)(4,1)} %bitcast.66), calls=%async_computation.4 | async-start | bytes 8388608
  263.9 33.9 %slice-start.4 = ((s8[9437184]{0:T(1024)(128)(4,1)}), s8[4194304]{0:T(1024)(128)(4,1)S(1)}, s32[]{:S(2)}) async-start(s8[9437184]{0:T(1024)(128)(4,1)} %bitcast.66), calls=%async_computation.5 | async-start | bytes 8388608
  263.9 33.8 %slice-start.5 = ((s8[9437184]{0:T(1024)(128)(4,1)}), s8[1048576]{0:T(1024)(128)(4,1)S(1)}, s32[]{:S(2)}) async-start(s8[9437184]{0:T(1024)(128)(4,1)} %bitcast.66), calls=%async_computation.6 | async-start | bytes 2097152
  263.9 33.8 %copy-start.5 = (f32[512,128]{1,0:T(8,128)S(1)}, f32[512,128]{1,0:T(8,128)}, u32[]{:S(2)}) copy-start(f32[512,128]{1,0:T(8,128)} %param.25) | copy-start | bytes 786436
  297.8 35.5 %copy-start.1 = (f32[1024,512]{1,0:T(8,128)S(1)}, f32[1024,512]{1,0:T(8,128)}, u32[]{:S(2)}) copy-start(f32[1024,512]{1,0:T(8,128)} %param.19) | copy-start | bytes 6291460
Sparse Core Ops, SparseCore 0:
  10.3 42.3 all-gather.6
